TPU v7x, 512 devices: a whole 4x8x8 slice. The times are simulated.
512 devices in a mesh: seq: 64 (over x, z, core), head: 8 (over y).
Axes of the slice: x: 4, y: 8, z: 8, core: 2. Of those that a mesh axis runs over, the one named last changes fastest.
Arguments:
- queries: bfloat16 [16384, 4096], P('seq', 'head'), may hold values from -6 to 6
- keys: bfloat16 [16384, 4096], P('seq', 'head'), may hold values from -6 to 6
- values: bfloat16 [16384, 4096], P('seq', 'head'), may hold values from -6 to 6
- gate: bfloat16 [16384, 4096], P('seq', 'head'), may hold values from -6 to 6
- residual: bfloat16 [16384, 4096], P('seq', 'head'), may hold values from -40 to 40
- log_decay: float32 [16384, 32], P('seq', 'head'), may hold values from -1 to 0, as said below
- out_weight: bfloat16 [4096, 4096], P('seq', 'head'), may hold values from -0.09375 to 0.09375
- norm_gain: bfloat16 [4096], P('head'), may hold values from 0.099609375 to 1.8984375
- kv_weight: bfloat16 [4096, 2048], P('seq', 'head'), may hold values from -0.09375 to 0.09375
Outputs:
- cache_keys: bfloat16 [16384, 1024], P('seq', 'head')
- cache_values: bfloat16 [16384, 1024], P('seq', 'head')
Inputs may be any that keep to these rules, and one draw needn't show every extreme that they name: `log_decay`: every entry is negative.
All inputs are finite; a program needn't handle non-finite values.
Results may differ from a plain program's by a relative error of at most 0.015.
Values may be sent and summed in bfloat16 or wider, within the bound.
A program may use at most 64 MiB of HBM per device.

v0:
```python
import jax
import jax.numpy as jnp
from jax import lax
from jax.sharding import PartitionSpec as P

HIGHEST = lax.Precision.HIGHEST


def entering(part, axis, combine, identity):
    place = lax.axis_index(axis)
    gathered = jax.tree.map(lambda a: lax.all_gather(a, axis), part)
    state = jax.tree.map(lambda a, e: jnp.zeros_like(a) + jnp.asarray(e, a.dtype), part, identity)

    def one(step, state):
        return combine(
            state, jax.tree.map(lambda a: lax.dynamic_index_in_dim(a, step, 0, False), gathered)
        )

    return lax.fori_loop(0, place, one, state)


def local_retention(queries, keys, values, log_decay, block):
    tokens, heads, width = queries.shape
    count = tokens // block

    def to_blocks(array):
        return array.reshape((count, block) + array.shape[1:])

    lower = jnp.arange(block)[:, None] >= jnp.arange(block)[None, :]

    def advance(carry, inputs):
        state, offset = carry
        query_block, key_block, value_block, decay_block = inputs
        within = jnp.cumsum(decay_block, axis=0)
        spread = within[:, None, :] - within[None, :, :]
        factor = jnp.where(
            lower[:, :, None], jnp.exp(jnp.where(lower[:, :, None], spread, 0.0)), 0.0
        )
        scores = jnp.einsum(
            "ihd,jhd->hij", query_block, key_block, preferred_element_type=jnp.float32
        )
        weighted = scores * jnp.transpose(factor, (2, 0, 1))
        values_wide = value_block.astype(jnp.float32)
        intra = jnp.einsum("hij,jhd->ihd", weighted, values_wide, precision=HIGHEST)
        query_wide = query_block.astype(jnp.float32)
        carried = jnp.exp(within)[:, :, None] * jnp.einsum(
            "ihd,hde->ihe", query_wide, state, precision=HIGHEST
        )
        ending = within[-1]
        key_wide = key_block.astype(jnp.float32) * jnp.exp(ending[None, :] - within)[:, :, None]
        fresh = jnp.exp(ending)[:, None, None] * state + jnp.einsum(
            "jhd,jhe->hde", key_wide, values_wide, precision=HIGHEST
        )
        return ((fresh, offset + ending), (intra + carried, offset[None, :] + within))

    start = (jnp.zeros((heads, width, width), jnp.float32), jnp.zeros((heads,), jnp.float32))
    final, stacked = lax.scan(
        advance,
        start,
        (to_blocks(queries), to_blocks(keys), to_blocks(values), to_blocks(log_decay)),
    )
    return (
        stacked[0].reshape(tokens, heads, width),
        stacked[1].reshape(tokens, heads),
        final[0],
        final[1],
    )


def combine_states(earlier, later):
    return (earlier[0] * later[0], later[0][:, None, None] * earlier[1] + later[1])


def on_device(queries, keys, values, gate, residual, log_decay, out_weight, norm_gain, kv_weight):
    tokens = queries.shape[0]
    heads = log_decay.shape[1]
    width = queries.shape[1] // heads
    shaped = [array.reshape(tokens, heads, width) for array in (queries, keys, values)]
    partial_out, running, state, offset = local_retention(
        shaped[0], shaped[1], shaped[2], log_decay, min(512, tokens)
    )
    identity = (jnp.ones((heads,), jnp.float32), jnp.zeros((heads, width, width), jnp.float32))
    scan_decay, incoming = entering((jnp.exp(offset), state), "seq", combine_states, identity)
    retained = partial_out + jnp.exp(running)[:, :, None] * jnp.einsum(
        "thd,hde->the", shaped[0].astype(jnp.float32), incoming, precision=HIGHEST
    )
    scale = lax.rsqrt(jnp.mean(retained * retained, axis=2, keepdims=True) + 1e-06)
    mixed = (
        jax.nn.silu(gate.astype(jnp.float32)) * (retained * scale).reshape(tokens, heads * width)
    ).astype(jnp.bfloat16)
    all_heads = lax.all_gather(mixed, "head", axis=1, tiled=True)
    out_full, kv_full = (
        lax.all_gather(out_weight, "seq", axis=0, tiled=True),
        lax.all_gather(kv_weight, "seq", axis=0, tiled=True),
    )
    branch = jnp.dot(all_heads, out_full, preferred_element_type=jnp.float32)
    hidden = (residual.astype(jnp.float32) + branch).astype(jnp.bfloat16)
    wide = hidden.astype(jnp.float32)
    squares = lax.psum(jnp.sum(wide * wide, axis=1), "head")
    features = wide.shape[1] * lax.axis_size("head")
    inverse = lax.rsqrt(squares[:, None] / features + 1e-06)
    local_norm = (wide * inverse * norm_gain.astype(jnp.float32)[None, :]).astype(jnp.bfloat16)
    normalized = lax.all_gather(local_norm, "head", axis=1, tiled=True)
    projected = jnp.dot(normalized, kv_full, preferred_element_type=jnp.float32)
    cache_heads = kv_weight.shape[1] // (2 * width)
    arranged = projected.reshape(tokens, cache_heads, 2, width)
    cache_keys = arranged[:, :, 0, :].reshape(tokens, cache_heads * width).astype(jnp.bfloat16)
    cache_values = arranged[:, :, 1, :].reshape(tokens, cache_heads * width).astype(jnp.bfloat16)
    return (cache_keys, cache_values)


def solution(mesh):
    placed = (
        P("seq", "head"),
        P("seq", "head"),
        P("seq", "head"),
        P("seq", "head"),
        P("seq", "head"),
        P("seq", "head"),
        P("seq", "head"),
        P("head"),
        P("seq", "head"),
    )
    return jax.shard_map(
        on_device,
        mesh=mesh,
        in_specs=placed,
        out_specs=(P("seq", "head"), P("seq", "head")),
        check_vma=False,
    )
```

profile of v0, /device:TPU:2, one launch (start us, length us, event | category | flops | bytes accessed | tf_op | source)
XLA Modules:
  0.0 390.9 jit_solution(8764286394529594663)
XLA Ops:
  7.2 0.7 reshape.72
  8.0 1.2 reduce-window.6
  9.2 0.1 slice.23
  9.2 0.1 copy.57
  9.4 0.1 copy.58
  9.5 0.1 add_bitcast_fusion
  9.6 0.2 slice_reduce_fusion
  9.8 0.1 bitcast_exponential_fusion
  9.8 1.1 copy.73
  10.9 2.0 convolution_add_fusion.1
  13.0 0.0 all-gather.10.cloned.1.call-start
  13.1 0.7 all-gather.10.cloned.1.call-update
  13.8 44.7 %all-gather.1 = f32[64,1,4]{2,1,0:T(1,128)S(1)} all-gather(f32[1,1,4]{2,1,0:T(1,128)S(1)} %bitcast.97), channel_id=1, replica_groups=mesh['seq'=64,'head'=8] {'seq'}, dimensions={0}, use_global_device_ids=true | all-gather | bytes 1040 | tf_op jit(solution)/shard_map/all_gather | solution.py:11
  58.6 0.4 fusion.2
  59.0 0.4 convolution_multiply_fusion
  59.4 63.1 %all-gather.16.cloned.1.call-done = f32[256,128,128]{2,1,0:T(8,128)} async-done(((f32[4,128,128]{2,1,0:T(8,128)}), f32[256,128,128]{2,1,0:T(8,128)}) %all-gather.16.cloned.1.call-update) | async-done | bytes 16777232 | tf_op jit(solution)/shard_map/all_gather | solution.py:11
  122.5 17.8 %while.3 = (s32[]{:T(128)}, f32[4,128,128]{2,1,0:T(8,128)S(1)}, s32[]{:T(128)}, f32[64,4]{1,0:T(8,128)S(1)}, f32[64,4,128,128]{3,2,1,0:T(8,128)}, /*index=5*/s32[]{:T(128)}, s32[]{:T(128)}, s32[]{:T(128)}) while((s32[]{:T(128)}, f32[4,128,128]{2,1,0:T(8,128)S(1)}, s32[]{:T(128)}, f32[64,4]{1,0:T(8,128)S(1)}, f32[64,4,128,128]{3,2,1,0:T(8,128)}, ...), condition=%wide.region_3.4_spmd, body=%wide.region_2.3_spmd.sunk | while | flops 131077 | bytes 786607 | solution.py:19
  122.6 1.1 bitcast_add_fusion.2
  123.7 1.1 bitcast_add_fusion.2
  124.8 1.1 bitcast_add_fusion.2
  125.9 1.1 bitcast_add_fusion.2
  127.0 1.1 bitcast_add_fusion.2
  128.1 1.1 bitcast_add_fusion.2
  129.2 1.1 bitcast_add_fusion.2
  130.4 1.1 bitcast_add_fusion.2
  131.5 1.1 bitcast_add_fusion.2
  132.6 1.1 bitcast_add_fusion.2
  133.7 1.1 bitcast_add_fusion.2
  134.8 1.1 bitcast_add_fusion.2
  135.9 1.1 bitcast_add_fusion.2
  137.0 1.1 bitcast_add_fusion.2
  138.1 1.1 bitcast_add_fusion.2
  139.2 1.1 bitcast_add_fusion.2
  140.3 0.4 fusion.3
  140.8 0.8 multiply_reduce_fusion.1
  141.6 0.2 copy.66
  141.8 0.9 fusion.12
  142.8 0.5 all-gather.14.cloned.1.call-update
  143.4 64.4 %all-gather.10.cloned.1.call-done = bf16[4096,512]{1,0:T(8,128)(2,1)} async-done(((bf16[64,512]{1,0:T(8,128)(2,1)}), bf16[4096,512]{1,0:T(8,128)(2,1)}) %all-gather.10.cloned.1.call-update) | async-done | bytes 4194320 | tf_op jit(solution)/shard_map/all_gather | solution.py:93
  207.8 43.4 %all-gather.8.cloned.1.call-done = bf16[256,4096]{1,0:T(8,128)(2,1)} async-done(((bf16[256,512]{1,0:T(8,128)(2,1)}), bf16[256,4096]{1,0:T(8,128)(2,1)}) %all-gather.8.cloned.1.call-update) | async-done | bytes 2097168 | tf_op jit(solution)/shard_map/all_gather | solution.py:91
  251.2 4.2 %multiply_reduce_fusion = (f32[256]{0:T(256)S(1)}, f32[256,512]{1,0:T(8,128)S(1)}) fusion(bf16[256,4096]{1,0:T(8,128)(2,1)} %all-gather.8.cloned.1.call-done, bf16[4096,512]{1,0:T(8,128)(2,1)} %all-gather.10.cloned.1.call-done, bf16[256,512]{1,0:T(8,128)(2,1)S(1)} %copy-done.4), kind=kOutput, calls=%fused_computation.22 | convolution fusion | flops 1074528000 | bytes 7078912 | tf_op jit(solution)/shard_map/dot_general | solution.py:96
  255.3 16.2 %psum.7 = f32[256]{0:T(256)S(1)} all-reduce(f32[256]{0:T(256)S(1)} %get-tuple-element.97), channel_id=1, replica_groups=mesh['seq'=64,'head'=8] {'head'}, use_global_device_ids=true, to_apply=%region_6.7 | all-reduce | flops 256 | bytes 2048 | tf_op jit(solution)/shard_map/psum | solution.py:99
  271.6 0.8 multiply_convert_fusion
  272.4 63.8 %all-gather.14.cloned.1.call-done = bf16[4096,256]{1,0:T(8,128)(2,1)} async-done(((bf16[64,256]{1,0:T(8,128)(2,1)}), bf16[4096,256]{1,0:T(8,128)(2,1)}) %all-gather.14.cloned.1.call-update) | async-done | bytes 2097168 | tf_op jit(solution)/shard_map/all_gather | solution.py:94
  336.2 43.6 %all-gather.12.cloned.1.call-done = bf16[256,4096]{1,0:T(8,128)(2,1)} async-done(((bf16[256,512]{1,0:T(8,128)(2,1)}), bf16[256,4096]{1,0:T(8,128)(2,1)}) %all-gather.12.cloned.1.call-update) | async-done | bytes 2097168 | tf_op jit(solution)/shard_map/all_gather | solution.py:103
  379.8 3.1 convolution_convert_fusion
  382.9 0.7 copy.71
  383.7 0.7 copy.72
  (44 shorter events, 0.6 us)
Async XLA Ops:
  7.2 51.4 %copy-start = (bf16[256,512]{1,0:T(8,128)(2,1)S(1)}, bf16[256,512]{1,0:T(8,128)(2,1)}, u32[]{:S(2)}) copy-start(bf16[256,512]{1,0:T(8,128)(2,1)} %param.11) | copy-start | bytes 786436
  7.2 115.3 %all-gather.16.cloned.1.call-start = ((), (), s32[]{:S(2)}) async-start(), calls=%async_computation.4 | async-start | bytes 17039360 | tf_op jit(solution)/shard_map/all_gather | solution.py:11
  13.0 194.8 %all-gather.10.cloned.1.call-start = ((), (), s32[]{:S(2)}) async-start(), calls=%async_computation.1 | async-start | bytes 4259840 | tf_op jit(solution)/shard_map/all_gather | solution.py:93
  13.8 237.4 %all-gather.8.cloned.1.call-start = ((), (), s32[]{:S(2)}) async-start(), calls=%async_computation | async-start | bytes 2359296 | tf_op jit(solution)/shard_map/all_gather | solution.py:91
  122.5 18.2 %copy-start.1 = (bf16[256,512]{1,0:T(8,128)(2,1)S(1)}, bf16[256,512]{1,0:T(8,128)(2,1)}, u32[]{:S(2)}) copy-start(bf16[256,512]{1,0:T(8,128)(2,1)} %param.13) | copy-start | bytes 786436
  140.8 1.1 copy-start.2
  141.5 1.8 copy-start.3
  141.5 109.7 %copy-start.4 = (bf16[256,512]{1,0:T(8,128)(2,1)S(1)}, bf16[256,512]{1,0:T(8,128)(2,1)}, u32[]{:S(2)}) copy-start(bf16[256,512]{1,0:T(8,128)(2,1)} %param.15) | copy-start | bytes 786436
  142.7 193.4 %all-gather.14.cloned.1.call-start = ((), (), s32[]{:S(2)}) async-start(), calls=%async_computation.3 | async-start | bytes 2129920 | tf_op jit(solution)/shard_map/all_gather | solution.py:94
  143.3 236.5 %all-gather.12.cloned.1.call-start = ((), (), s32[]{:S(2)}) async-start(), calls=%async_computation.2 | async-start | bytes 2359296 | tf_op jit(solution)/shard_map/all_gather | solution.py:103
Sparse Core Ops, SparseCore 0:
  13.1 109.3 all-gather.15
  125.8 81.8 all-gather.9
  209.9 41.2 all-gather.7
  254.4 81.7 all-gather.13
  338.1 41.6 all-gather.11
where the time goes:
time: 393 us; the launch traced here: 391 us
  waiting for transfers between devices  280 us (71%)
  blocking collectives  60.9 us (15%)
  other arithmetic  20.2 us (5%)
  between operations  14 us (4%)
  matrix products  11.3 us (3%)
  local copies, waits for them, and re-layouts  4.19 us (1%)
    all_gather x1, waiting for transfers between devices, on_device(): lax.all_gather(out_weight, 'seq', axis=0, tiled=True)  64.4 us
    all_gather x1, waiting for transfers between devices, on_device(): lax.all_gather(kv_weight, 'seq', axis=0, tiled=True)  63.8 us
    all_gather x1, waiting for transfers between devices, entering(): gathered = jax.tree.map(lambda a: lax.all_gather(a, axis), part)  63.1 us
    all_gather x1, blocking collectives, entering(): gathered = jax.tree.map(lambda a: lax.all_gather(a, axis), part)  44.7 us
    all_gather x1, waiting for transfers between devices, on_device(): normalized = lax.all_gather(local_norm, 'head', axis=1, tiled=True)  43.6 us
    all_gather x1, waiting for transfers between devices, on_device(): all_heads = lax.all_gather(mixed, 'head', axis=1, tiled=True)  43.4 us
    add x16, other arithmetic, combine_states(): later[0][:, None, None] * earlier[1] + later[1]  17 us
    psum x1, blocking collectives, on_device(): squares = lax.psum(jnp.sum(wide * wide, axis=1), 'head')  16.2 us
  transfers between devices with their start and end apart: 5, of which 5 were waited for; matrix products, arithmetic and copies ran while one was open for 6% of the time, Pallas kernels for 0%

commit v1 on v0

--- a/solution.py
+++ b/solution.py
@@ -90,7 +90,9 @@
     ).astype(jnp.bfloat16)
     all_heads = lax.all_gather(mixed, "head", axis=1, tiled=True)
     out_full, kv_full = (
-        lax.all_gather(out_weight, "seq", axis=0, tiled=True),
+        jnp.concatenate(
+            lax.all_to_all(jnp.stack([out_weight] * lax.axis_size("seq")), "seq", 0, 0), axis=0
+        ),
         lax.all_gather(kv_weight, "seq", axis=0, tiled=True),
     )
     branch = jnp.dot(all_heads, out_full, preferred_element_type=jnp.float32)

time: 393 us -> 439 us (1.12)
  blocking collectives: 60.9 us -> 172 us
  waiting for transfers between devices: 280 us -> 197 us
  starting transfers between devices: 0.2 us -> 14.2 us
    all_gather x1, blocking collectives: 44.7 us -> 156 us  [entering(): gathered = jax.tree.map(lambda a: lax.all_gather(a, axis), part)]
    all_gather x1 -> x0, waiting for transfers between devices: 64.4 us -> none  [on_device(): lax.all_gather(out_weight, 'seq', axis=0, tiled=True)]
    all_gather x1, waiting for transfers between devices: 63.1 us -> 0.02 us  [entering(): gathered = jax.tree.map(lambda a: lax.all_gather(a, axis), part)]
    all_gather x1, waiting for transfers between devices: 43.4 us -> 89 us  [on_device(): all_heads = lax.all_gather(mixed, 'head', axis=1, tiled=True)]
    all_to_all x0 -> x1, starting transfers between devices: none -> 14.1 us  [on_device(): lax.all_to_all(jnp.stack([out_weight] * lax.axis_size('seq')), 'seq', 0, 0)]
  transfers between devices with their start and end apart: 5 -> 5, of which waited for: 5 -> 3; matrix products, arithmetic and copies ran while one was open for 6% -> 7% of each run, Pallas kernels for 0% -> 0%
where the time goes in v1:
time: 439 us; the launch traced here: 437 us
  waiting for transfers between devices  197 us (45%)
  blocking collectives  172 us (39%)
  other arithmetic  20.2 us (5%)
  starting transfers between devices  14.2 us (3%)
  between operations  14 us (3%)
  matrix products  11.3 us (3%)
  local copies, waits for them, and re-layouts  7.5 us (2%)
    all_gather x1, blocking collectives, entering(): gathered = jax.tree.map(lambda a: lax.all_gather(a, axis), part)  156 us
    all_gather x1, waiting for transfers between devices, on_device(): all_heads = lax.all_gather(mixed, 'head', axis=1, tiled=True)  89 us
    all_gather x1, waiting for transfers between devices, on_device(): lax.all_gather(kv_weight, 'seq', axis=0, tiled=True)  63.9 us
    all_gather x1, waiting for transfers between devices, on_device(): normalized = lax.all_gather(local_norm, 'head', axis=1, tiled=True)  43.6 us
    add x16, other arithmetic, combine_states(): later[0][:, None, None] * earlier[1] + later[1]  17 us
    psum x1, blocking collectives, on_device(): squares = lax.psum(jnp.sum(wide * wide, axis=1), 'head')  16.2 us
    all_to_all x1, starting transfers between devices, on_device(): lax.all_to_all(jnp.stack([out_weight] * lax.axis_size('seq')), 'seq', 0, 0)  14.1 us
  transfers between devices with their start and end apart: 5, of which 3 were waited for; matrix products, arithmetic and copies ran while one was open for 7% of the time, Pallas kernels for 0%

profile of v1, /device:TPU:2, one launch (start us, length us, event | category | flops | bytes accessed | tf_op | source)
XLA Modules:
  0.0 436.9 jit_solution(14107692007055989667)
XLA Ops:
  7.2 0.7 reshape.77
  8.0 1.2 reduce-window.6
  9.2 0.1 slice.23
  9.2 0.1 copy.57
  9.4 0.1 copy.58
  9.5 0.1 add_bitcast_fusion
  9.6 0.2 slice_reduce_fusion
  9.8 0.1 bitcast_exponential_fusion
  9.8 1.1 copy.73
  10.9 2.1 convolution_add_fusion.1
  13.0 3.3 stack.2
  16.3 14.1 %all-to-all-start = ((bf16[64,64,512]{2,1,0:T(8,128)(2,1)}), bf16[64,64,512]{2,1,0:T(8,128)(2,1)}, u32[]{:S(2)}, u32[]{:S(2)}) async-start(bf16[64,64,512]{2,1,0:T(8,128)(2,1)} %stack.2), calls=%async_computation | async-start | bytes 8388608 | tf_op jit(solution)/shard_map/all_to_all | solution.py:94
  30.4 0.0 all-gather.7.cloned.1.call-start
  30.5 155.7 %all-gather.1 = f32[64,1,4]{2,1,0:T(1,128)S(1)} all-gather(f32[1,1,4]{2,1,0:T(1,128)S(1)} %bitcast.98), channel_id=1, replica_groups=mesh['seq'=64,'head'=8] {'seq'}, dimensions={0}, use_global_device_ids=true | all-gather | bytes 1040 | tf_op jit(solution)/shard_map/all_gather | solution.py:11
  186.2 0.4 fusion.2
  186.6 0.4 convolution_multiply_fusion
  187.0 17.7 %while.3 = (s32[]{:T(128)}, f32[4,128,128]{2,1,0:T(8,128)S(1)}, s32[]{:T(128)}, f32[64,4]{1,0:T(8,128)S(1)}, f32[64,4,128,128]{3,2,1,0:T(8,128)}, /*index=5*/s32[]{:T(128)}, s32[]{:T(128)}, s32[]{:T(128)}) while((s32[]{:T(128)}, f32[4,128,128]{2,1,0:T(8,128)S(1)}, s32[]{:T(128)}, f32[64,4]{1,0:T(8,128)S(1)}, f32[64,4,128,128]{3,2,1,0:T(8,128)}, ...), condition=%wide.region_3.4_spmd, body=%wide.region_2.3_spmd.sunk | while | flops 131077 | bytes 786607 | solution.py:19
  187.1 1.1 bitcast_add_fusion.2
  188.2 1.1 bitcast_add_fusion.2
  189.3 1.1 bitcast_add_fusion.2
  190.4 1.1 bitcast_add_fusion.2
  191.5 1.1 bitcast_add_fusion.2
  192.6 1.1 bitcast_add_fusion.2
  193.7 1.1 bitcast_add_fusion.2
  194.9 1.1 bitcast_add_fusion.2
  196.0 1.1 bitcast_add_fusion.2
  197.1 1.1 bitcast_add_fusion.2
  198.2 1.1 bitcast_add_fusion.2
  199.3 1.1 bitcast_add_fusion.2
  200.4 1.1 bitcast_add_fusion.2
  201.5 1.1 bitcast_add_fusion.2
  202.6 1.1 bitcast_add_fusion.2
  203.7 1.1 bitcast_add_fusion.2
  204.8 0.4 fusion.3
  205.2 0.8 multiply_reduce_fusion.1
  206.1 0.2 copy.66
  206.3 0.9 fusion.12
  207.2 0.0 all-gather.11.cloned.1.call-start
  207.2 0.7 all-gather.11.cloned.1.call-update
  208.0 89.0 %all-gather.7.cloned.1.call-done = bf16[256,4096]{1,0:T(8,128)(2,1)} async-done(((bf16[256,512]{1,0:T(8,128)(2,1)}), bf16[256,4096]{1,0:T(8,128)(2,1)}) %all-gather.7.cloned.1.call-update) | async-done | bytes 2097168 | tf_op jit(solution)/shard_map/all_gather | solution.py:91
  297.0 4.1 multiply_reduce_fusion
  301.1 16.2 %psum.7 = f32[256]{0:T(256)S(1)} all-reduce(f32[256]{0:T(256)S(1)} %get-tuple-element.97), channel_id=1, replica_groups=mesh['seq'=64,'head'=8] {'head'}, use_global_device_ids=true, to_apply=%region_6.7 | all-reduce | flops 256 | bytes 2048 | tf_op jit(solution)/shard_map/psum | solution.py:101
  317.4 0.8 multiply_convert_fusion
  318.2 63.9 %all-gather.11.cloned.1.call-done = bf16[4096,256]{1,0:T(8,128)(2,1)} async-done(((bf16[64,256]{1,0:T(8,128)(2,1)}), bf16[4096,256]{1,0:T(8,128)(2,1)}) %all-gather.11.cloned.1.call-update) | async-done | bytes 2097168 | tf_op jit(solution)/shard_map/all_gather | solution.py:96
  382.1 43.6 %all-gather.9.cloned.1.call-done = bf16[256,4096]{1,0:T(8,128)(2,1)} async-done(((bf16[256,512]{1,0:T(8,128)(2,1)}), bf16[256,4096]{1,0:T(8,128)(2,1)}) %all-gather.9.cloned.1.call-update) | async-done | bytes 2097168 | tf_op jit(solution)/shard_map/all_gather | solution.py:105
  425.7 3.1 convolution_convert_fusion
  428.9 0.7 copy.71
  429.6 0.7 copy.72
  (44 shorter events, 0.5 us)
Async XLA Ops:
  7.2 179.0 %copy-start = (bf16[256,512]{1,0:T(8,128)(2,1)S(1)}, bf16[256,512]{1,0:T(8,128)(2,1)}, u32[]{:S(2)}) copy-start(bf16[256,512]{1,0:T(8,128)(2,1)} %param.11) | copy-start | bytes 786436
  7.2 179.8 %all-gather.13.cloned.1.call-start = ((), (), s32[]{:S(2)}) async-start(), calls=%async_computation.4 | async-start | bytes 17039360 | tf_op jit(solution)/shard_map/all_gather | solution.py:11
  16.3 191.6 %all-to-all-start = ((bf16[64,64,512]{2,1,0:T(8,128)(2,1)}), bf16[64,64,512]{2,1,0:T(8,128)(2,1)}, u32[]{:S(2)}, u32[]{:S(2)}) async-start(bf16[64,64,512]{2,1,0:T(8,128)(2,1)} %stack.2), calls=%async_computation | async-start | bytes 8388608 | tf_op jit(solution)/shard_map/all_to_all | solution.py:94
  30.4 266.6 %all-gather.7.cloned.1.call-start = ((), (), s32[]{:S(2)}) async-start(), calls=%async_computation.1 | async-start | bytes 2359296 | tf_op jit(solution)/shard_map/all_gather | solution.py:91
  187.0 18.2 %copy-start.1 = (bf16[256,512]{1,0:T(8,128)(2,1)S(1)}, bf16[256,512]{1,0:T(8,128)(2,1)}, u32[]{:S(2)}) copy-start(bf16[256,512]{1,0:T(8,128)(2,1)} %param.13) | copy-start | bytes 786436
  205.2 1.1 copy-start.2
  206.0 2.0 copy-start.3
  206.0 91.0 %copy-start.4 = (bf16[256,512]{1,0:T(8,128)(2,1)S(1)}, bf16[256,512]{1,0:T(8,128)(2,1)}, u32[]{:S(2)}) copy-start(bf16[256,512]{1,0:T(8,128)(2,1)} %param.15) | copy-start | bytes 786436
  207.2 174.9 %all-gather.11.cloned.1.call-start = ((), (), s32[]{:S(2)}) async-start(), calls=%async_computation.3 | async-start | bytes 2129920 | tf_op jit(solution)/shard_map/all_gather | solution.py:96
  207.9 217.8 %all-gather.9.cloned.1.call-start = ((), (), s32[]{:S(2)}) async-start(), calls=%async_computation.2 | async-start | bytes 2359296 | tf_op jit(solution)/shard_map/all_gather | solution.py:105
Sparse Core Ops, SparseCore 0:
  13.2 161.8 all-gather.12
  207.3 89.6 all-gather.6
  300.4 81.7 all-gather.10
  384.0 41.6 all-gather.8
